TPU v7x, 32 devices: a whole 2x2x4 slice. The times are simulated.
32 devices in a mesh: fsdp: 8 (over z, y), ctx: 4 (over x, core).
Axes of the slice: x: 2, y: 2, z: 4, core: 2. Of those that a mesh axis runs over, the one named last changes fastest.
Arguments:
- tokens: bfloat16 [8, 1024, 2048], P('fsdp', 'ctx'), may hold values from -6 to 6
- norm_gain: bfloat16 [2048], P('fsdp'), may hold values from 0.5 to 1.5
- w_in: bfloat16 [2048, 8512], P('fsdp'), may hold values from -0.125 to 0.125
- conv_w: bfloat16 [4, 4352], P(None, 'fsdp'), may hold values from -3 to 3
- conv_b: bfloat16 [4352], P('fsdp'), may hold values from -0.5 to 0.5
- dt_bias: float32 [64], replicated, may hold values from -4.5 to -3
- a_log: float32 [64], replicated, may hold values from -7 to 0.5
- d_skip: float32 [64], replicated, may hold values from 0.5 to 2
- gate_gain: bfloat16 [4096], P('fsdp'), may hold values from 0.5 to 1.5
- w_out: bfloat16 [4096, 2048], P('fsdp'), may hold values from -0.09375 to 0.09375
- cotangent: bfloat16 [8, 1024, 2048], P('fsdp', 'ctx'), may hold values from -6 to 6
Outputs:
- output: bfloat16 [8, 1024, 2048], P('fsdp', 'ctx')
- grad_tokens: float32 [8, 1024, 2048], P('fsdp', 'ctx')
- grad_norm_gain: float32 [2048], P('fsdp')
- grad_w_in: float32 [2048, 8512], P('fsdp')
- grad_conv_w: float32 [4, 4352], P(None, 'fsdp')
- grad_conv_b: float32 [4352], P('fsdp')
- grad_dt_bias: float32 [64], replicated
- grad_a_log: float32 [64], replicated
- grad_d_skip: float32 [64], replicated
- grad_gate_gain: float32 [4096], P('fsdp')
- grad_w_out: float32 [4096, 2048], P('fsdp')
All inputs are finite; a program needn't handle non-finite values.
Results may differ from a plain program's by a relative error of at most 0.0085.
The roundings to bfloat16 on the way count: a program that leaves them out, or rounds other values in their place, can miss the bound.
Values may be sent and summed in bfloat16 or wider, within the bound.
No kernel may reach another device: no remote copies, remote signals or barrier semaphores. Data moves between devices by JAX's collectives and lax.ppermute only.
A program may use at most 320 MiB of HBM per device.

v0:
```python
import jax
import jax.numpy as jnp
from jax import lax
from jax.sharding import PartitionSpec as P

HEADS = 64
HEADDIM = 64
STATE = 128
KW = 4
GROUP = 256
CONV = 4352
EPS = 1e-05


def passed_along(block, axis, distance):
    devices = range(lax.axis_size(axis))
    route = [(i - distance, i) for i in devices if i - distance in devices]
    return lax.ppermute(block, axis, route)


def carried_in(part, axis, combine, identity, reverse):
    count = lax.axis_size(axis)
    place = lax.axis_index(axis)
    ahead = count - 1 - place if reverse else place
    gathered = jax.tree.map(lambda a: lax.all_gather(a, axis), part)
    state = jax.tree.map(lambda a, e: jnp.zeros_like(a) + jnp.asarray(e, a.dtype), part, identity)

    def one(turn, state):
        source = count - 1 - turn if reverse else turn
        return combine(
            state, jax.tree.map(lambda a: lax.dynamic_index_in_dim(a, source, 0, False), gathered)
        )

    return lax.fori_loop(0, ahead, one, state)


def in_norm(values, gain_vec):
    inverse = lax.rsqrt(jnp.mean(values * values, axis=-1, keepdims=True) + EPS)
    return values * inverse * gain_vec


def gate_norm(ssd_out, gate_z, gain_vec):
    gated = ssd_out * jax.nn.silu(gate_z)
    inverse = lax.rsqrt(jnp.mean(gated * gated, axis=-1, keepdims=True) + EPS)
    return gated * inverse * gain_vec


def conv_silu(padded, taps, offsets_bias):
    length = padded.shape[0] - taps.shape[0] + 1
    summed = offsets_bias[None, :] + taps[0][None, :] * padded[0:length]
    for offset in range(1, taps.shape[0]):
        summed = summed + taps[offset][None, :] * padded[offset : offset + length]
    return jax.nn.silu(summed)


def decay_matrix(cumulative):
    count = cumulative.shape[0]
    row_index = lax.broadcasted_iota(jnp.int32, (count, count), 0)
    col_index = lax.broadcasted_iota(jnp.int32, (count, count), 1)
    lower = (row_index >= col_index)[None]
    differ = cumulative.T[:, :, None] - cumulative.T[:, None, :]
    return jnp.where(lower, jnp.exp(jnp.where(lower, differ, 0.0)), 0.0)


def block_weighted(b_block, cumulative, step_sizes):
    tail_vals = jnp.exp(cumulative[-1][None, :] - cumulative) * step_sizes
    weighted = (tail_vals.T[:, :, None] * b_block.astype(jnp.float32)[None]).astype(jnp.bfloat16)
    return (tail_vals, weighted)


def link_states(earlier, later):
    return (earlier[0] * later[0], later[0][:, None, None] * earlier[1] + later[1])


def body(
    tokens, norm_gain, w_in, conv_w, conv_b, dt_bias, a_log, d_skip, gate_gain, w_out, cotangent
):
    gathered = (
        lax.all_gather(norm_gain, "fsdp", axis=0, tiled=True),
        lax.all_gather(w_in, "fsdp", axis=0, tiled=True),
        lax.all_gather(conv_w, "fsdp", axis=1, tiled=True),
        lax.all_gather(conv_b, "fsdp", axis=0, tiled=True),
        lax.all_gather(gate_gain, "fsdp", axis=0, tiled=True),
        lax.all_gather(w_out, "fsdp", axis=0, tiled=True),
    )
    norm_full, w_in_full, conv_w_full, conv_b_full, gate_full, w_out_full = gathered
    inputs = tokens[0].astype(jnp.float32)
    length = inputs.shape[0]
    inner_width = HEADS * HEADDIM
    blocks = length // GROUP
    normed_f, norm_back = jax.vjp(in_norm, inputs, norm_full.astype(jnp.float32))
    normed = normed_f.astype(jnp.bfloat16)
    proj = jnp.dot(normed, w_in_full, preferred_element_type=jnp.float32).astype(jnp.bfloat16)
    gate_z = proj[:, :inner_width].astype(jnp.float32)
    conv_in = proj[:, inner_width : inner_width + CONV]
    dt_raw = proj[:, inner_width + CONV :].astype(jnp.float32)
    halo_rows = passed_along(conv_in[length - KW + 1 :], "ctx", 1)
    padded = jnp.concatenate([halo_rows, conv_in], axis=0).astype(jnp.float32)
    activated, conv_back_fn = jax.vjp(
        conv_silu, padded, conv_w_full.astype(jnp.float32), conv_b_full.astype(jnp.float32)
    )
    act_low = activated.astype(jnp.bfloat16)
    x_all = act_low[:, :inner_width].reshape(blocks, GROUP, HEADS, HEADDIM)
    b_all = act_low[:, inner_width : inner_width + STATE].reshape(blocks, GROUP, STATE)
    c_all = act_low[:, inner_width + STATE :].reshape(blocks, GROUP, STATE)
    dt_in = dt_raw + dt_bias[None, :]
    step_sizes = jax.nn.softplus(dt_in)
    a_neg = -jnp.exp(a_log)
    step_all = step_sizes.reshape(blocks, GROUP, HEADS)
    piece_log = jnp.sum(step_sizes * a_neg[None, :], axis=0)
    zero_state = jnp.zeros((HEADS, HEADDIM, STATE), jnp.float32)

    def cumulate(step_block):
        return jnp.cumsum(step_block * a_neg[None, :], axis=0)

    def state_step(state, pieces):
        x_block, b_block, step_block = pieces
        cumulative = cumulate(step_block)
        tail_vals, weighted = block_weighted(b_block, cumulative, step_block)
        local = jnp.einsum("jhp,hjn->hpn", x_block, weighted, preferred_element_type=jnp.float32)
        return (jnp.exp(cumulative[-1])[:, None, None] * state + local, None)

    end_state, unused = lax.scan(state_step, zero_state, (x_all, b_all, step_all))
    identity = (jnp.ones((HEADS,), jnp.float32), zero_state)
    prefix = carried_in((jnp.exp(piece_log), end_state), "ctx", link_states, identity, False)
    start_state = prefix[1]

    def forward_step(state, pieces):
        x_block, b_block, c_block, step_block = pieces
        cumulative = cumulate(step_block)
        gram = jnp.einsum("in,jn->ij", c_block, b_block, preferred_element_type=jnp.float32)
        scores = (gram[None] * decay_matrix(cumulative) * step_block.T[:, None, :]).astype(
            jnp.bfloat16
        )
        intra = jnp.einsum("hij,jhp->ihp", scores, x_block, preferred_element_type=jnp.float32)
        inner = jnp.einsum(
            "in,hpn->ihp", c_block, state.astype(jnp.bfloat16), preferred_element_type=jnp.float32
        )
        tail_vals, weighted = block_weighted(b_block, cumulative, step_block)
        local = jnp.einsum("jhp,hjn->hpn", x_block, weighted, preferred_element_type=jnp.float32)
        new_state = jnp.exp(cumulative[-1])[:, None, None] * state + local
        return (new_state, (intra + jnp.exp(cumulative)[:, :, None] * inner, state))

    unused_end, (block_out, block_starts) = lax.scan(
        forward_step, start_state, (x_all, b_all, c_all, step_all)
    )
    xs_float = x_all.reshape(length, HEADS, HEADDIM).astype(jnp.float32)
    ssd_out = (
        block_out.reshape(length, HEADS, HEADDIM) + d_skip[None, :, None] * xs_float
    ).reshape(length, inner_width)
    mixed_f, gate_back = jax.vjp(gate_norm, ssd_out, gate_z, gate_full.astype(jnp.float32))
    mixed = mixed_f.astype(jnp.bfloat16)
    branch = jnp.dot(mixed, w_out_full, preferred_element_type=jnp.float32)
    output = (inputs + branch).astype(jnp.bfloat16)[None]
    regathered = (
        lax.all_gather(norm_gain, "fsdp", axis=0, tiled=True),
        lax.all_gather(w_in, "fsdp", axis=0, tiled=True),
        lax.all_gather(conv_w, "fsdp", axis=1, tiled=True),
        lax.all_gather(conv_b, "fsdp", axis=0, tiled=True),
        lax.all_gather(gate_gain, "fsdp", axis=0, tiled=True),
        lax.all_gather(w_out, "fsdp", axis=0, tiled=True),
    )
    w_in_full = regathered[1]
    w_out_full = regathered[5]
    seed = cotangent[0]
    d_w_out = jnp.einsum("td,te->de", mixed, seed, preferred_element_type=jnp.float32)
    d_mixed = jnp.einsum("te,de->td", seed, w_out_full, preferred_element_type=jnp.float32)
    d_ssd_f, d_gate_z, d_gate_gain = gate_back(d_mixed)
    d_ssd = d_ssd_f.astype(jnp.bfloat16)
    d_ssd3 = d_ssd.astype(jnp.float32).reshape(length, HEADS, HEADDIM)
    d_skip_grad = jnp.sum(d_ssd3 * xs_float, axis=(0, 2))
    d_all = d_ssd.reshape(blocks, GROUP, HEADS, HEADDIM)

    def grad_state_step(carried, pieces):
        c_block, step_block, d_block = pieces
        cumulative = cumulate(step_block)
        d_inner = (d_block.astype(jnp.float32) * jnp.exp(cumulative)[:, :, None]).astype(
            jnp.bfloat16
        )
        from_out = jnp.einsum("ihp,in->hpn", d_inner, c_block, preferred_element_type=jnp.float32)
        return (jnp.exp(cumulative[-1])[:, None, None] * carried + from_out, None)

    grad_local, unused = lax.scan(
        grad_state_step, zero_state, (c_all, step_all, d_all), reverse=True
    )
    identity_back = (jnp.ones((HEADS,), jnp.float32), zero_state)
    suffix = carried_in((jnp.exp(piece_log), grad_local), "ctx", link_states, identity_back, True)
    end_grad = suffix[1]

    def grad_step(carried, pieces):
        x_block, b_block, c_block, step_block, d_block, state = pieces
        b_float = b_block.astype(jnp.float32)
        d_float = d_block.astype(jnp.float32)
        cumulative = cumulate(step_block)
        last_decay = jnp.exp(cumulative[-1])
        tail_vals, weighted = block_weighted(b_block, cumulative, step_block)
        d_state = last_decay[:, None, None] * carried
        d_last = jnp.sum(carried * state, axis=(1, 2)) * last_decay
        d_local = carried.astype(jnp.bfloat16)
        d_x = jnp.einsum("hjn,hpn->jhp", weighted, d_local, preferred_element_type=jnp.float32)
        d_weighted = jnp.einsum(
            "jhp,hpn->hjn", x_block, d_local, preferred_element_type=jnp.float32
        )
        d_b = jnp.sum(d_weighted * tail_vals.T[:, :, None], axis=0)
        d_tail = jnp.sum(d_weighted * b_float[None], axis=2).T
        d_step = d_tail * jnp.exp(cumulative[-1][None, :] - cumulative)
        tail_log = d_tail * tail_vals
        d_last = d_last + jnp.sum(tail_log, axis=0)
        d_cum = -tail_log
        growth = jnp.exp(cumulative)
        state_low = state.astype(jnp.bfloat16)
        inner = jnp.einsum("in,hpn->ihp", c_block, state_low, preferred_element_type=jnp.float32)
        d_cum = d_cum + jnp.sum(d_float * inner, axis=2) * growth
        d_inner = (d_float * growth[:, :, None]).astype(jnp.bfloat16)
        d_c = jnp.einsum("ihp,hpn->in", d_inner, state_low, preferred_element_type=jnp.float32)
        d_state = d_state + jnp.einsum(
            "ihp,in->hpn", d_inner, c_block, preferred_element_type=jnp.float32
        )
        gram = jnp.einsum("in,jn->ij", c_block, b_block, preferred_element_type=jnp.float32)
        decays = decay_matrix(cumulative)
        step_cols = step_block.T[:, None, :]
        scores = (gram[None] * decays * step_cols).astype(jnp.bfloat16)
        d_scores = jnp.einsum("ihp,jhp->hij", d_block, x_block, preferred_element_type=jnp.float32)
        d_x = d_x + jnp.einsum("hij,ihp->jhp", scores, d_block, preferred_element_type=jnp.float32)
        common = d_scores * decays
        d_gram = jnp.sum(common * step_cols, axis=0).astype(jnp.bfloat16)
        d_step = d_step + jnp.sum(common * gram[None], axis=1).T
        exponent = common * gram[None] * step_cols
        d_cum = d_cum + jnp.sum(exponent, axis=2).T - jnp.sum(exponent, axis=1).T
        d_c = d_c + jnp.einsum("ij,jn->in", d_gram, b_block, preferred_element_type=jnp.float32)
        d_b = d_b + jnp.einsum("ij,in->jn", d_gram, c_block, preferred_element_type=jnp.float32)
        last_row = lax.broadcasted_iota(jnp.int32, d_cum.shape, 0) == d_cum.shape[0] - 1
        d_cum = d_cum + jnp.where(last_row, d_last[None, :], 0.0)
        d_rate = jnp.cumsum(d_cum[::-1], axis=0)[::-1]
        return (d_state, (d_x, d_b, d_c, d_step, d_rate))

    unused_grad, block_grads = lax.scan(
        grad_step, end_grad, (x_all, b_all, c_all, step_all, d_all, block_starts), reverse=True
    )
    d_x_all, d_b_all, d_c_all, d_step_all, d_rate_all = block_grads
    d_rate_flat = d_rate_all.reshape(length, HEADS)
    d_x_flat = (d_x_all.reshape(length, HEADS, HEADDIM) + d_skip[None, :, None] * d_ssd3).reshape(
        length, inner_width
    )
    d_act = jnp.concatenate(
        [d_x_flat, d_b_all.reshape(length, STATE), d_c_all.reshape(length, STATE)], axis=1
    )
    d_padded, d_conv_w, d_conv_b = conv_back_fn(d_act)
    returned = passed_along(d_padded[: KW - 1].astype(jnp.bfloat16), "ctx", -1).astype(jnp.float32)
    d_conv_in = d_padded[KW - 1 :] + jnp.concatenate(
        [jnp.zeros((length - KW + 1, CONV), jnp.float32), returned], axis=0
    )
    d_step_total = d_step_all.reshape(length, HEADS) + d_rate_flat * a_neg[None, :]
    d_dt_in = d_step_total * jax.nn.sigmoid(dt_in)
    d_dt_bias = jnp.sum(d_dt_in, axis=0)
    d_a_log = jnp.sum(d_rate_flat * step_sizes, axis=0) * a_neg
    d_proj = jnp.concatenate([d_gate_z, d_conv_in, d_dt_in], axis=1).astype(jnp.bfloat16)
    d_w_in = jnp.einsum("td,tk->dk", normed, d_proj, preferred_element_type=jnp.float32)
    d_normed = jnp.einsum("tk,dk->td", d_proj, w_in_full, preferred_element_type=jnp.float32)
    d_inputs, d_norm_gain = norm_back(d_normed)
    grad_tokens = (seed.astype(jnp.float32) + d_inputs)[None]
    shares = (
        lax.psum_scatter(d_norm_gain, "fsdp", scatter_dimension=0, tiled=True),
        lax.psum_scatter(d_w_in, "fsdp", scatter_dimension=0, tiled=True),
        lax.psum_scatter(d_conv_w, "fsdp", scatter_dimension=1, tiled=True),
        lax.psum_scatter(d_conv_b, "fsdp", scatter_dimension=0, tiled=True),
        lax.psum_scatter(d_gate_gain, "fsdp", scatter_dimension=0, tiled=True),
        lax.psum_scatter(d_w_out, "fsdp", scatter_dimension=0, tiled=True),
    )
    summed = lax.psum((shares[0], shares[1], shares[2], shares[3], shares[4], shares[5]), "ctx")
    head_sums = lax.psum((d_dt_bias, d_a_log, d_skip_grad), ("fsdp", "ctx"))
    return (
        output,
        grad_tokens,
        summed[0],
        summed[1],
        summed[2],
        summed[3],
        head_sums[0],
        head_sums[1],
        head_sums[2],
        summed[4],
        summed[5],
    )


def solution(mesh):
    in_specs = (
        P("fsdp", "ctx", None),
        P("fsdp"),
        P("fsdp", None),
        P(None, "fsdp"),
        P("fsdp"),
        P(),
        P(),
        P(),
        P("fsdp"),
        P("fsdp", None),
        P("fsdp", "ctx", None),
    )
    out_specs = (
        P("fsdp", "ctx", None),
        P("fsdp", "ctx", None),
        P("fsdp"),
        P("fsdp", None),
        P(None, "fsdp"),
        P("fsdp"),
        P(),
        P(),
        P(),
        P("fsdp"),
        P("fsdp", None),
    )
    return jax.shard_map(body, mesh=mesh, in_specs=in_specs, out_specs=out_specs, check_vma=False)
```

profile of v0, /device:TPU:0, one launch (start us, length us, event | category | flops | bytes accessed | tf_op | source)
XLA Modules:
  0.0 3068.2 jit_solution(707199861307095639)
XLA Ops:
  8.1 63.6 %all-gather.4 = bf16[8,1,256]{2,1,0:T(2,128)(2,1)S(1)} all-gather(bf16[1,1,256]{2,1,0:T(2,128)(2,1)S(1)} %reshape.249), channel_id=1, replica_groups=mesh['fsdp'=8,'ctx'=4] {'fsdp'}, dimensions={0}, use_global_device_ids=true | all-gather | bytes 4608 | tf_op jit(solution)/shard_map/all_gather | solution.py:79
  71.7 30.6 all-gather.3
  104.0 75.0 %all-reduce.9 = bf16[4352]{0:T(1024)(128)(2,1)S(1)} all-reduce(bf16[4352]{0:T(1024)(128)(2,1)S(1)} %dynamic-update-slice), channel_id=1, replica_groups=mesh['fsdp'=8,'ctx'=4] {'fsdp'}, use_global_device_ids=true, to_apply=%add.9 | all-reduce | flops 4352 | bytes 17408
  179.6 498.4 %all-gather.11.cloned.1.call-done = bf16[2048,8512]{0,1:T(8,128)(2,1)} async-done(((bf16[256,8512]{0,1:T(8,128)(2,1)}), bf16[2048,8512]{0,1:T(8,128)(2,1)}) %all-gather.11.cloned.1.call-update) | async-done | bytes 34865168 | tf_op jit(solution)/shard_map/all_gather | solution.py:80
  678.0 17.2 convolution_convert_fusion
  718.4 26.6 all-gather.5
  745.7 6.1 all-reduce.10
  752.5 23.1 all-gather.15.cloned.1.call-done
  777.8 6.8 bitcast_add_fusion.2
  784.6 6.1 copy.140
  790.7 5.9 multiply_reduce_fusion.12
  797.8 207.6 %all-gather.13.cloned.1.call-done = bf16[4096,2048]{1,0:T(8,128)(2,1)} async-done(((bf16[512,2048]{1,0:T(8,128)(2,1)}), bf16[4096,2048]{1,0:T(8,128)(2,1)}) %all-gather.13.cloned.1.call-update) | async-done | bytes 16777232 | tf_op jit(solution)/shard_map/all_gather | solution.py:84
  1005.4 20.1 multiply_reduce_fusion.10
  1026.2 9.7 fusion.12
  1043.9 17.6 fusion.48
  1062.5 12.5 multiply_reduce_fusion.2
  1082.9 7.7 fusion.1
  1090.6 9.7 all-gather.17.cloned.1.call-done
  1101.8 13.9 while.17
  1130.7 5.8 copy.143
  1140.8 6.4 multiply_reduce_fusion.9
  1152.5 6.3 pad_add_fusion
  1162.6 26.9 fusion.39
  1192.0 455.4 %reduce-scatter.8.cloned.1.call-done = f32[512,2048]{1,0:T(8,128)} async-done(((f32[4096,2048]{1,0:T(8,128)}), f32[512,2048]{1,0:T(8,128)}) %reduce-scatter.8.cloned.1.call-update) | async-done | bytes 4194320 | tf_op jit(solution)/shard_map/reduce_scatter | solution.py:268
  1647.4 1103.3 %reduce-scatter.6.cloned.1.call-done = f32[256,8512]{0,1:T(8,128)} async-done(((f32[2048,8512]{0,1:T(8,128)}), f32[256,8512]{0,1:T(8,128)}) %reduce-scatter.6.cloned.1.call-update) | async-done | bytes 8716304 | tf_op jit(solution)/shard_map/reduce_scatter | solution.py:264
  2753.0 12.6 fusion.27
  2765.6 39.7 %all-reduce.14 = (f32[64]{0:T(128)}, f32[64]{0:T(128)}, f32[64]{0:T(128)}) all-reduce(f32[64]{0:T(128)S(1)} %get-tuple-element.299, f32[64]{0:T(128)S(1)} %fusion.83, f32[64]{0:T(128)S(1)} %reduce_sum.298), channel_id=1, replica_groups=mesh['fsdp'=8,'ctx'=4] {'fsdp','ctx'}, use_global_device_ids=true, to_apply=%region_37.38 | all-reduce | flops 192 | bytes 1536 | tf_op jit(solution)/shard_map/psum | solution.py:271
  2805.2 17.6 fusion.30
  2822.9 37.4 %all-reduce.15 = (f32[2048]{0:T(1024)S(1)}, f32[4352]{0:T(1024)S(1)}, f32[4096]{0:T(1024)S(1)}) all-reduce(f32[2048]{0:T(1024)S(1)} %get-tuple-element.259, f32[4352]{0:T(1024)S(1)} %get-tuple-element.258, f32[4096]{0:T(1024)S(1)} %copy-done.39), channel_id=5, replica_groups=mesh['fsdp'=8,'ctx'=4] {'fsdp'}, use_global_device_ids=true, to_apply=%region_23.24.clone | all-reduce | flops 10496 | bytes 83968
  2865.6 12.8 all-reduce.16
  2878.4 173.4 %all-reduce.20.cloned.1.call-done = (f32[256,8512]{0,1:T(8,128)}, f32[512,2048]{1,0:T(8,128)}) async-done(((f32[256,8512]{0,1:T(8,128)}, f32[512,2048]{1,0:T(8,128)}), (f32[256,8512]{0,1:T(8,128)}, f32[512,2048]{1,0:T(8,128)})) %all-reduce.20.cloned.1.call-update) | async-done | bytes 12910608 | tf_op jit(solution)/shard_map/psum | solution.py:270
  3051.7 6.8 copy.186
  (256 shorter events, 100.1 us)
Async XLA Ops:
  7.2 95.2 %copy-start.46 = (u32[32]{0:T(128)S(1)}, u32[32]{0:T(128)}, u32[]{:S(2)}) copy-start(u32[32]{0:T(128)} %constant.172) | copy-start | bytes 388
  7.2 64.4 %copy-start.43 = (bf16[4,544]{1,0:T(4,128)(2,1)S(1)}, bf16[4,544]{1,0:T(4,128)(2,1)}, u32[]{:S(2)}) copy-start(bf16[4,544]{1,0:T(4,128)(2,1)} %param.18) | copy-start | bytes 13060
  7.2 96.5 %copy-start.48 = (bf16[544]{0:T(1024)(128)(2,1)S(1)}, bf16[544]{0:T(1024)(128)(2,1)}, u32[]{:S(2)}) copy-start(bf16[544]{0:T(1024)(128)(2,1)} %param.19) | copy-start | bytes 3268
  7.2 172.0 %copy-start.5 = (bf16[1,256,2048]{2,1,0:T(8,128)(2,1)S(1)}, bf16[1,256,2048]{2,1,0:T(8,128)(2,1)}, u32[]{:S(2)}) copy-start(bf16[1,256,2048]{2,1,0:T(8,128)(2,1)} %param.15) | copy-start | bytes 3145732
  7.2 172.3 %copy-start.58 = (f32[64]{0:T(128)S(1)}, f32[64]{0:T(128)}, u32[]{:S(2)}) copy-start(f32[64]{0:T(128)} %param.21) | copy-start | bytes 772
  7.2 670.7 %all-gather.11.cloned.1.call-start = ((), (), s32[]{:S(2)}) async-start(), calls=%async_computation.3 | async-start | bytes 39223296 | tf_op jit(solution)/shard_map/all_gather | solution.py:80
  8.0 767.6 %all-gather.15.cloned.1.call-start = ((), (), s32[]{:S(2)}) async-start(), calls=%async_computation.7 | async-start | bytes 10485760 | tf_op jit(solution)/shard_map/all_gather | solution.py:25
  71.6 606.3 %copy-start.10 = (f32[8,1,256]{2,1,0:T(1,128)}, f32[8,1,256]{2,1,0:T(1,128)S(1)}, u32[]{:S(2)}) copy-start(f32[8,1,256]{2,1,0:T(1,128)S(1)} %convert_element_type.136) | copy-start | bytes 24580
  179.2 522.2 %copy-start.21 = (f32[4352]{0:T(1024)}, f32[4352]{0:T(1024)S(1)}, u32[]{:S(2)}) copy-start(f32[4352]{0:T(1024)S(1)} %get-tuple-element.261) | copy-start | bytes 52228
  179.2 522.2 %copy-start.23 = (f32[4352]{0:T(1024)}, f32[4352]{0:T(1024)S(1)}, u32[]{:S(2)}) copy-start(f32[4352]{0:T(1024)S(1)} %get-tuple-element.262) | copy-start | bytes 52228
  179.2 522.2 %copy-start.25 = (f32[4352]{0:T(1024)}, f32[4352]{0:T(1024)S(1)}, u32[]{:S(2)}) copy-start(f32[4352]{0:T(1024)S(1)} %get-tuple-element.263) | copy-start | bytes 52228
  179.2 522.2 %copy-start.27 = (f32[4352]{0:T(1024)}, f32[4352]{0:T(1024)S(1)}, u32[]{:S(2)}) copy-start(f32[4352]{0:T(1024)S(1)} %get-tuple-element.264) | copy-start | bytes 52228
  179.5 498.4 %copy-start.40 = (f32[256]{0:T(256)}, f32[256]{0:T(256)S(1)}, u32[]{:S(2)}) copy-start(f32[256]{0:T(256)S(1)} %fusion.33) | copy-start | bytes 3076
  179.6 518.1 %copy-start.49 = (f32[64]{0:T(128)}, f32[64]{0:T(128)S(1)}, u32[]{:S(2)}) copy-start(f32[64]{0:T(128)S(1)} %exponential_negate_fusion) | copy-start | bytes 772
  179.6 498.4 %copy-start.12 = (f32[256]{0:T(256)}, f32[256]{0:T(256)S(1)}, u32[]{:S(2)}) copy-start(f32[256]{0:T(256)S(1)} %fusion.76) | copy-start | bytes 3076
  678.0 19.8 copy-start.44
  696.2 4.7 collective-permute-start
  705.7 46.6 %copy-start.1 = (bf16[256,4352]{1,0:T(8,128)(2,1)}, bf16[256,4352]{1,0:T(8,128)(2,1)S(1)}, u32[]{:S(2)}) copy-start(bf16[256,4352]{1,0:T(8,128)(2,1)S(1)} %get-tuple-element.304) | copy-start | bytes 6684676
  716.2 289.2 %all-gather.13.cloned.1.call-start = ((), (), s32[]{:S(2)}) async-start(), calls=%async_computation.4 | async-start | bytes 18874368 | tf_op jit(solution)/shard_map/all_gather | solution.py:84
  717.0 383.3 %all-gather.17.cloned.1.call-start = ((), (), s32[]{:S(2)}) async-start(), calls=%async_computation.8 | async-start | bytes 10485760 | tf_op jit(solution)/shard_map/all_gather | solution.py:25
  745.6 32.1 %copy-start.36 = (pred[256,256]{1,0:T(8,128)(4,1)}, pred[256,256]{1,0:T(8,128)(4,1)S(1)}, u32[]{:S(2)}) copy-start(pred[256,256]{1,0:T(8,128)(4,1)S(1)} %iota_compare_fusion) | copy-start | bytes 196612
  752.1 25.7 copy-start.30
  752.2 25.6 copy-start.33
  752.3 25.5 copy-start.17
  752.5 25.3 copy-start.19
  790.7 214.7 %copy-start.8 = (bf16[1,256,2048]{2,1,0:T(8,128)(2,1)S(1)}, bf16[1,256,2048]{2,1,0:T(8,128)(2,1)}, u32[]{:S(2)}) copy-start(bf16[1,256,2048]{2,1,0:T(8,128)(2,1)} %param.25) | copy-start | bytes 3145732
  1043.7 603.7 %reduce-scatter.8.cloned.1.call-start = ((), (), s32[]{:S(2)}) async-start(), calls=%async_computation.6 | async-start | bytes 37748736 | tf_op jit(solution)/shard_map/reduce_scatter | solution.py:268
  1061.6 1689.1 %reduce-scatter.6.cloned.1.call-start = ((), (), s32[]{:S(2)}) async-start(), calls=%async_computation.5 | async-start | bytes 78446592 | tf_op jit(solution)/shard_map/reduce_scatter | solution.py:264
  1158.9 3.2 collective-permute-start.1
  1189.5 1675.0 %reduce-scatter.10.cloned.1.call-start = ((), (), s32[]{:S(2)}) async-start(), calls=%async_computation.9 | async-start | bytes 2506752
  1191.9 1859.8 %all-reduce.20.cloned.1.call-start = ((), (), s32[]{:S(2)}) async-start(), calls=%async_computation.10 | async-start | bytes 25821184 | tf_op jit(solution)/shard_map/psum | solution.py:270
  2805.2 55.3 %copy-start.41 = (f32[256]{0:T(256)S(1)}, f32[256]{0:T(256)}, u32[]{:S(2)}) copy-start(f32[256]{0:T(256)} %copy-done.40) | copy-start | bytes 3076
  (42 other events, 228.8 us)
Sparse Core Ops, SparseCore 0:
  9.5 668.3 all-gather.10
  716.3 59.2 all-gather.14
  777.7 227.6 all-gather.12
  1043.8 56.4 all-gather.16
  1103.9 543.4 reduce-scatter.7
  1651.1 1099.4 reduce-scatter.5
  2755.1 67.8 reduce-scatter.9
  2825.9 225.8 all-reduce.19
where the time goes:
time: 3080 us; the launch traced here: 3070 us
  waiting for transfers between devices  2470 us (80%)
  blocking collectives  292 us (9%)
  matrix products  164 us (5%)
  other arithmetic  70 us (2%)
  local copies, waits for them, and re-layouts  46.4 us (2%)
    reduce_scatter x1, waiting for transfers between devices, body(): lax.psum_scatter(d_w_in, 'fsdp', scatter_dimension=0, tiled=True)  1100 us
    all_gather x1, waiting for transfers between devices, body(): lax.all_gather(w_in, 'fsdp', axis=0, tiled=True)  498 us
    reduce_scatter x1, waiting for transfers between devices, body(): lax.psum_scatter(d_w_out, 'fsdp', scatter_dimension=0, tiled=True)  455 us
    all_gather x1, waiting for transfers between devices, body(): lax.all_gather(w_out, 'fsdp', axis=0, tiled=True)  208 us
    psum x1, waiting for transfers between devices, body(): lax.psum((shares[0], shares[1], shares[2], shares[3], shares[4], shares[5...  173 us
    unnamed x3, blocking collectives  119 us
    all_gather x1, blocking collectives, body(): lax.all_gather(norm_gain, 'fsdp', axis=0, tiled=True)  63.6 us
  transfers between devices with their start and end apart: 10, of which 8 were waited for; matrix products, arithmetic and copies ran while one was open for 6% of the time, Pallas kernels for 0%

commit v1 on v0

--- a/solution.py
+++ b/solution.py
@@ -12,6 +12,24 @@
 EPS = 1e-05
 
 
+def collect(shard, axis, dim):
+    ways, here, step = (lax.axis_size(axis), lax.axis_index(axis), shard.shape[dim])
+    dims = [n * ways if d == dim else n for d, n in enumerate(shard.shape)]
+    full = lax.dynamic_update_slice_in_dim(
+        jnp.zeros(dims, shard.dtype), shard, here * step, axis=dim
+    )
+    going_up = going_down = shard
+    for far in range(1, ways // 2 + 1):
+        going_up = lax.ppermute(going_up, axis, [(d, (d + 1) % ways) for d in range(ways)])
+        full = lax.dynamic_update_slice_in_dim(full, going_up, (here - far) % ways * step, axis=dim)
+        if 2 * far < ways:
+            going_down = lax.ppermute(going_down, axis, [(d, (d - 1) % ways) for d in range(ways)])
+            full = lax.dynamic_update_slice_in_dim(
+                full, going_down, (here + far) % ways * step, axis=dim
+            )
+    return full
+
+
 def passed_along(block, axis, distance):
     devices = range(lax.axis_size(axis))
     route = [(i - distance, i) for i in devices if i - distance in devices]
@@ -77,7 +95,7 @@
 ):
     gathered = (
         lax.all_gather(norm_gain, "fsdp", axis=0, tiled=True),
-        lax.all_gather(w_in, "fsdp", axis=0, tiled=True),
+        collect(w_in, "fsdp", 0),
         lax.all_gather(conv_w, "fsdp", axis=1, tiled=True),
         lax.all_gather(conv_b, "fsdp", axis=0, tiled=True),
         lax.all_gather(gate_gain, "fsdp", axis=0, tiled=True),

time: 3080 us -> 3810 us (1.24)
  waiting for transfers between devices: 2470 us -> 2990 us
  blocking collectives: 292 us -> 457 us
  local copies, waits for them, and re-layouts: 46.4 us -> 86.1 us
    ppermute x0 -> x7, waiting for transfers between devices: none -> 350 us  [the longest x4 184 us: collect(): lax.ppermute(going_up, axis, [(d, (d + 1) % ways) for d in range(ways)])]
    all_gather x1, waiting for transfers between devices: 498 us -> 663 us  [body(): lax.all_gather(w_in, 'fsdp', axis=0, tiled=True)]
    all_gather x1, blocking collectives: 63.6 us -> 197 us  [body(): lax.all_gather(norm_gain, 'fsdp', axis=0, tiled=True)]
  transfers between devices with their start and end apart: 10 -> 17, of which waited for: 8 -> 11; matrix products, arithmetic and copies ran while one was open for 6% -> 6% of each run, Pallas kernels for 0% -> 0%
where the time goes in v1:
time: 3810 us
  waiting for transfers between devices  2990 us (78%)
  blocking collectives  457 us (12%)
  matrix products  165 us (4%)
  local copies, waits for them, and re-layouts  86.1 us (2%)
  other arithmetic  71.9 us (2%)
    reduce_scatter x1, waiting for transfers between devices, body(): lax.psum_scatter(d_w_in, 'fsdp', scatter_dimension=0, tiled=True)  1100 us
    all_gather x1, waiting for transfers between devices, body(): lax.all_gather(w_in, 'fsdp', axis=0, tiled=True)  663 us
    reduce_scatter x1, waiting for transfers between devices, body(): lax.psum_scatter(d_w_out, 'fsdp', scatter_dimension=0, tiled=True)  454 us
    all_gather x1, waiting for transfers between devices, body(): lax.all_gather(w_out, 'fsdp', axis=0, tiled=True)  208 us
    all_gather x1, blocking collectives, body(): lax.all_gather(norm_gain, 'fsdp', axis=0, tiled=True)  197 us
    ppermute x4, waiting for transfers between devices, collect(): lax.ppermute(going_up, axis, [(d, (d + 1) % ways) for d in range(ways)])  184 us
    ppermute x3, waiting for transfers between devices, collect(): lax.ppermute(going_down, axis, [(d, (d - 1) % ways) for d in range(ways)])  166 us
    psum x1, waiting for transfers between devices, body(): lax.psum((shares[0], shares[1], shares[2], shares[3], shares[4], shares[5...  160 us
  transfers between devices with their start and end apart: 17, of which 11 were waited for; matrix products, arithmetic and copies ran while one was open for 6% of the time, Pallas kernels for 0%

profile of v1, /device:TPU:0, one launch (start us, length us, event | category | flops | bytes accessed | tf_op | source)
XLA Modules:
  0.0 3805.1 jit_solution(12126986416169650047)
XLA Ops:
  13.3 183.9 %collective-permute-done = bf16[256,8512]{0,1:T(8,128)(2,1)} collective-permute-done((bf16[256,8512]{0,1:T(8,128)(2,1)}, bf16[256,8512]{0,1:T(8,128)(2,1)}, u32[]{:S(2)}, u32[]{:S(2)}) %collective-permute-start) | collective-permute-done | bytes 4358176 | tf_op jit(solution)/shard_map/ppermute | solution.py:23
  203.5 197.4 %all-gather.4 = bf16[8,1,256]{2,1,0:T(2,128)(2,1)S(1)} all-gather(bf16[1,1,256]{2,1,0:T(2,128)(2,1)S(1)} %reshape.249), channel_id=1, replica_groups=mesh['fsdp'=8,'ctx'=4] {'fsdp'}, dimensions={0}, use_global_device_ids=true | all-gather | bytes 4608 | tf_op jit(solution)/shard_map/all_gather | solution.py:97
  400.9 30.9 all-gather.3
  434.9 110.1 %all-reduce.9 = bf16[4352]{0:T(1024)(128)(2,1)S(1)} all-reduce(bf16[4352]{0:T(1024)(128)(2,1)S(1)} %dynamic-update-slice), channel_id=1, replica_groups=mesh['fsdp'=8,'ctx'=4] {'fsdp'}, use_global_device_ids=true, to_apply=%add.9 | all-reduce | flops 4352 | bytes 17408
  547.7 11.6 broadcast_in_dim.168
  582.9 165.7 %collective-permute-done.5 = bf16[256,8512]{0,1:T(8,128)(2,1)S(1)} collective-permute-done((bf16[256,8512]{0,1:T(8,128)(2,1)}, bf16[256,8512]{0,1:T(8,128)(2,1)S(1)}, u32[]{:S(2)}, u32[]{:S(2)}) %collective-permute-start.5) | collective-permute-done | bytes 4358176 | tf_op jit(solution)/shard_map/ppermute | solution.py:26
  753.1 17.3 convolution_convert_fusion
  793.5 26.0 all-gather.5
  827.2 21.1 all-gather.15.cloned.1.call-done
  850.3 6.8 bitcast_add_fusion.2
  870.2 207.8 %all-gather.11.cloned.1.call-done = bf16[4096,2048]{1,0:T(8,128)(2,1)} async-done(((bf16[512,2048]{1,0:T(8,128)(2,1)}), bf16[4096,2048]{1,0:T(8,128)(2,1)}) %all-gather.11.cloned.1.call-update) | async-done | bytes 16777232 | tf_op jit(solution)/shard_map/all_gather | solution.py:102
  1078.0 20.1 multiply_reduce_fusion.10
  1098.8 9.7 fusion.12
  1116.6 17.6 fusion.48
  1135.2 12.5 multiply_reduce_fusion.2
  1155.5 7.7 fusion.1
  1163.2 9.7 all-gather.17.cloned.1.call-done
  1174.5 13.9 while.17
  1213.5 6.5 multiply_reduce_fusion.9
  1225.2 6.3 pad_add_fusion
  1235.2 26.9 fusion.39
  1265.4 454.4 %reduce-scatter.8.cloned.1.call-done = f32[512,2048]{1,0:T(8,128)} async-done(((f32[4096,2048]{1,0:T(8,128)}), f32[512,2048]{1,0:T(8,128)}) %reduce-scatter.8.cloned.1.call-update) | async-done | bytes 4194320 | tf_op jit(solution)/shard_map/reduce_scatter | solution.py:286
  1719.8 1102.7 %reduce-scatter.6.cloned.1.call-done = f32[256,8512]{0,1:T(8,128)} async-done(((f32[2048,8512]{0,1:T(8,128)}), f32[256,8512]{0,1:T(8,128)}) %reduce-scatter.6.cloned.1.call-update) | async-done | bytes 8716304 | tf_op jit(solution)/shard_map/reduce_scatter | solution.py:282
  2824.8 12.6 fusion.27
  2837.4 39.6 %all-reduce.14 = (f32[64]{0:T(128)}, f32[64]{0:T(128)}, f32[64]{0:T(128)}) all-reduce(f32[64]{0:T(128)S(1)} %get-tuple-element.299, f32[64]{0:T(128)S(1)} %fusion.83, f32[64]{0:T(128)S(1)} %reduce_sum.298), channel_id=1, replica_groups=mesh['fsdp'=8,'ctx'=4] {'fsdp','ctx'}, use_global_device_ids=true, to_apply=%region_37.38 | all-reduce | flops 192 | bytes 1536 | tf_op jit(solution)/shard_map/psum | solution.py:289
  2877.0 17.6 reduce-scatter.10.cloned.1.call-done
  2895.7 663.2 %all-gather.13.cloned.1.call-done = bf16[2048,8512]{0,1:T(8,128)(2,1)} async-done(((bf16[256,8512]{0,1:T(8,128)(2,1)}), bf16[2048,8512]{0,1:T(8,128)(2,1)}) %all-gather.13.cloned.1.call-update) | async-done | bytes 34865168 | tf_op jit(solution)/shard_map/all_gather | solution.py:175
  3558.9 18.9 fusion.30
  3577.8 34.5 all-reduce.15
  3612.6 12.5 all-reduce.16
  3628.9 159.7 %all-reduce.20.cloned.1.call-done = (f32[256,8512]{0,1:T(8,128)}, f32[512,2048]{1,0:T(8,128)}) async-done(((f32[256,8512]{0,1:T(8,128)}, f32[512,2048]{1,0:T(8,128)}), (f32[256,8512]{0,1:T(8,128)}, f32[512,2048]{1,0:T(8,128)})) %all-reduce.20.cloned.1.call-update) | async-done | bytes 12910608 | tf_op jit(solution)/shard_map/psum | solution.py:288
  3788.6 6.8 copy.194
  (274 shorter events, 167.6 us)
Async XLA Ops:
  7.2 841.1 %all-gather.15.cloned.1.call-start = ((), (), s32[]{:S(2)}) async-start(), calls=%async_computation.7 | async-start | bytes 10485760 | tf_op jit(solution)/shard_map/all_gather | solution.py:43
  7.2 190.1 %collective-permute-start = (bf16[256,8512]{0,1:T(8,128)(2,1)}, bf16[256,8512]{0,1:T(8,128)(2,1)}, u32[]{:S(2)}, u32[]{:S(2)}) collective-permute-start(bf16[256,8512]{0,1:T(8,128)(2,1)} %param.17), channel_id=1, source_target_pairs={{0,4},{4,8},{8,12},{12,16},{16,20},{20,24},{24,28},{28,0},{1,5},{5... | collective-permute-start | bytes 13074440 | tf_op jit(solution)/shard_map/ppermute | solution.py:23
  10.2 189.5 %collective-permute-start.1 = (bf16[256,8512]{0,1:T(8,128)(2,1)}, bf16[256,8512]{0,1:T(8,128)(2,1)}, u32[]{:S(2)}, u32[]{:S(2)}) collective-permute-start(bf16[256,8512]{0,1:T(8,128)(2,1)} %param.17), channel_id=1, source_target_pairs={{0,28},{4,0},{8,4},{12,8},{16,12},{20,16},{24,20},{28,24},{1,29},{... | collective-permute-start | bytes 13074440 | tf_op jit(solution)/shard_map/ppermute | solution.py:26
  197.3 234.5 %collective-permute-start.2 = (bf16[256,8512]{0,1:T(8,128)(2,1)}, bf16[256,8512]{0,1:T(8,128)(2,1)}, u32[]{:S(2)}, u32[]{:S(2)}) collective-permute-start(bf16[256,8512]{0,1:T(8,128)(2,1)} %collective-permute-done), channel_id=1, source_target_pairs={{0,4},{4,8},{8,12},{12,16},{16,20},{20,24},{24,28},{28,0},{1,5},{5... | collective-permute-start | bytes 13074440 | tf_op jit(solution)/shard_map/ppermute | solution.py:23
  199.8 365.6 %collective-permute-start.3 = (bf16[256,8512]{0,1:T(8,128)(2,1)}, bf16[256,8512]{0,1:T(8,128)(2,1)}, u32[]{:S(2)}, u32[]{:S(2)}) collective-permute-start(bf16[256,8512]{0,1:T(8,128)(2,1)} %collective-permute-done.1), channel_id=1, source_target_pairs={{0,28},{4,0},{8,4},{12,8},{16,12},{20,16},{24,20},{28,24},{1,29},{... | collective-permute-start | bytes 13074440 | tf_op jit(solution)/shard_map/ppermute | solution.py:26
  400.9 352.2 %copy-start.10 = (f32[8,1,256]{2,1,0:T(1,128)}, f32[8,1,256]{2,1,0:T(1,128)S(1)}, u32[]{:S(2)}) copy-start(f32[8,1,256]{2,1,0:T(1,128)S(1)} %convert_element_type.136) | copy-start | bytes 24580
  431.8 137.4 %collective-permute-start.4 = (bf16[256,8512]{0,1:T(8,128)(2,1)}, bf16[256,8512]{0,1:T(8,128)(2,1)}, u32[]{:S(2)}, u32[]{:S(2)}) collective-permute-start(bf16[256,8512]{0,1:T(8,128)(2,1)} %collective-permute-done.2), channel_id=1, source_target_pairs={{0,4},{4,8},{8,12},{12,16},{16,20},{20,24},{24,28},{28,0},{1,5},{5... | collective-permute-start | bytes 13074440 | tf_op jit(solution)/shard_map/ppermute | solution.py:23
  545.2 231.2 %copy-start.21 = (f32[4352]{0:T(1024)}, f32[4352]{0:T(1024)S(1)}, u32[]{:S(2)}) copy-start(f32[4352]{0:T(1024)S(1)} %get-tuple-element.261) | copy-start | bytes 52228
  545.3 231.2 %copy-start.23 = (f32[4352]{0:T(1024)}, f32[4352]{0:T(1024)S(1)}, u32[]{:S(2)}) copy-start(f32[4352]{0:T(1024)S(1)} %get-tuple-element.262) | copy-start | bytes 52228
  545.3 231.2 %copy-start.25 = (f32[4352]{0:T(1024)}, f32[4352]{0:T(1024)S(1)}, u32[]{:S(2)}) copy-start(f32[4352]{0:T(1024)S(1)} %get-tuple-element.263) | copy-start | bytes 52228
  545.3 231.2 %copy-start.27 = (f32[4352]{0:T(1024)}, f32[4352]{0:T(1024)S(1)}, u32[]{:S(2)}) copy-start(f32[4352]{0:T(1024)S(1)} %get-tuple-element.264) | copy-start | bytes 52228
  547.6 225.2 %copy-start.46 = (f32[64]{0:T(128)}, f32[64]{0:T(128)S(1)}, u32[]{:S(2)}) copy-start(f32[64]{0:T(128)S(1)} %exponential_negate_fusion) | copy-start | bytes 772
  547.6 205.5 %copy-start.12 = (f32[256]{0:T(256)}, f32[256]{0:T(256)S(1)}, u32[]{:S(2)}) copy-start(f32[256]{0:T(256)S(1)} %fusion.76) | copy-start | bytes 3076
  565.4 183.2 %collective-permute-start.5 = (bf16[256,8512]{0,1:T(8,128)(2,1)}, bf16[256,8512]{0,1:T(8,128)(2,1)S(1)}, u32[]{:S(2)}, u32[]{:S(2)}) collective-permute-start(bf16[256,8512]{0,1:T(8,128)(2,1)} %collective-permute-done.3), channel_id=1, source_target_pairs={{0,28},{4,0},{8,4},{12,8},{16,12},{20,16},{24,20},{28,24},{1,29},{... | collective-permute-start | bytes 13074440 | tf_op jit(solution)/shard_map/ppermute | solution.py:26
  569.3 181.5 %collective-permute-start.6 = (bf16[256,8512]{0,1:T(8,128)(2,1)}, bf16[256,8512]{0,1:T(8,128)(2,1)S(1)}, u32[]{:S(2)}, u32[]{:S(2)}) collective-permute-start(bf16[256,8512]{0,1:T(8,128)(2,1)} %collective-permute-done.4), channel_id=1, source_target_pairs={{0,4},{4,8},{8,12},{12,16},{16,20},{20,24},{24,28},{28,0},{1,5},{5... | collective-permute-start | bytes 13074440 | tf_op jit(solution)/shard_map/ppermute | solution.py:23
  771.5 4.5 collective-permute-start.7
  780.7 46.2 %copy-start.1 = (bf16[256,4352]{1,0:T(8,128)(2,1)}, bf16[256,4352]{1,0:T(8,128)(2,1)S(1)}, u32[]{:S(2)}) copy-start(bf16[256,4352]{1,0:T(8,128)(2,1)S(1)} %get-tuple-element.304) | copy-start | bytes 6684676
  791.3 286.7 %all-gather.11.cloned.1.call-start = ((), (), s32[]{:S(2)}) async-start(), calls=%async_computation.3 | async-start | bytes 18874368 | tf_op jit(solution)/shard_map/all_gather | solution.py:102
  792.1 380.9 %all-gather.17.cloned.1.call-start = ((), (), s32[]{:S(2)}) async-start(), calls=%async_computation.8 | async-start | bytes 10485760 | tf_op jit(solution)/shard_map/all_gather | solution.py:43
  820.2 30.1 copy-start.36
  826.8 23.5 copy-start.30
  826.9 23.4 copy-start.33
  827.0 23.3 copy-start.17
  863.2 214.8 %copy-start.8 = (bf16[1,256,2048]{2,1,0:T(8,128)(2,1)S(1)}, bf16[1,256,2048]{2,1,0:T(8,128)(2,1)}, u32[]{:S(2)}) copy-start(bf16[1,256,2048]{2,1,0:T(8,128)(2,1)} %param.25) | copy-start | bytes 3145732
  1116.3 603.5 %reduce-scatter.8.cloned.1.call-start = ((), (), s32[]{:S(2)}) async-start(), calls=%async_computation.6 | async-start | bytes 37748736 | tf_op jit(solution)/shard_map/reduce_scatter | solution.py:286
  1134.2 1688.3 %reduce-scatter.6.cloned.1.call-start = ((), (), s32[]{:S(2)}) async-start(), calls=%async_computation.5 | async-start | bytes 78446592 | tf_op jit(solution)/shard_map/reduce_scatter | solution.py:282
  1231.6 3.2 collective-permute-start.8
  1262.1 1632.5 %reduce-scatter.10.cloned.1.call-start = ((), (), s32[]{:S(2)}) async-start(), calls=%async_computation.9 | async-start | bytes 2506752
  1264.6 2294.3 %all-gather.13.cloned.1.call-start = ((), (), s32[]{:S(2)}) async-start(), calls=%async_computation.4 | async-start | bytes 39223296 | tf_op jit(solution)/shard_map/all_gather | solution.py:175
  1265.3 2523.3 %all-reduce.20.cloned.1.call-start = ((), (), s32[]{:S(2)}) async-start(), calls=%async_computation.10 | async-start | bytes 25821184 | tf_op jit(solution)/shard_map/psum | solution.py:288
  2895.7 682.1 %copy-start.39 = (f32[4096]{0:T(1024)S(1)}, f32[4096]{0:T(1024)}, u32[]{:S(2)}) copy-start(f32[4096]{0:T(1024)} %get-tuple-element.254) | copy-start | bytes 49156
  2895.7 729.4 %copy-start.41 = (f32[256]{0:T(256)S(1)}, f32[256]{0:T(256)}, u32[]{:S(2)}) copy-start(f32[256]{0:T(256)} %copy-done.40) | copy-start | bytes 3076
  (46 other events, 293.2 us)
Sparse Core Ops, SparseCore 0:
  791.4 56.7 all-gather.14
  850.4 227.6 all-gather.10
  1116.4 56.4 all-gather.16
  1176.5 543.1 reduce-scatter.7
  1723.5 1098.9 reduce-scatter.5
  2826.8 67.7 reduce-scatter.9
  2896.1 662.7 all-gather.12
  3561.7 226.8 all-reduce.19
